TPU v7x, 32 devices: a whole 2x2x4 slice. The times are simulated.
32 devices in a mesh: blk: 4 (over y, x), dp: 8 (over z, core).
Axes of the slice: x: 2, y: 2, z: 4, core: 2. Of those that a mesh axis runs over, the one named last changes fastest.
Arguments:
- patches: bfloat16 [4096, 64, 256], P(('blk', 'dp')), may hold values from -6 to 6
- w_mix: bfloat16 [256, 128], replicated, may hold values from -0.375 to 0.375
- w_in: bfloat16 [2048, 512], replicated, may hold values from -0.125 to 0.125
- w_out: bfloat16 [512, 128], replicated, may hold values from -0.25 to 0.25
- partner_dev: int32 [4096], P(('blk', 'dp')), may hold values from 0 to 7, as said below
- partner_row: int32 [4096], P(('blk', 'dp')), may hold values from 0 to 127, as said below
Outputs:
- loss_rows: float32 [4096], P(('blk', 'dp'))
- grad_mix: float32 [256, 128], replicated
- grad_in: float32 [2048, 512], replicated
- grad_out: float32 [512, 128], replicated
Inputs may be any that keep to these rules, and one draw needn't show every extreme that they name: Among one device's rows every dp index appears as partner_dev exactly 128/8 times. Over the rows that share a blk index, the pairs (partner_dev, partner_row) name every pair of dp index and row of a device exactly once.
All inputs are finite; a program needn't handle non-finite values.
Results may differ from a plain program's by a relative error of at most 0.012.
The roundings to bfloat16 on the way count: a program that leaves them out, or rounds other values in their place, can miss the bound.
Values may be sent and summed in bfloat16 or wider, within the bound.
No kernel may reach another device: no remote copies, remote signals or barrier semaphores. Data moves between devices by JAX's collectives and lax.ppermute only.
A program may use at most 64 MiB of HBM per device.

v0:
```python
import math
import jax
import jax.numpy as jnp
from jax import lax
from jax.sharding import PartitionSpec as P

SCALE = 10.0


def dft_table(length, freqs):
    angle_idx = jnp.arange(length, dtype=jnp.int32)
    freq_idx = jnp.arange(freqs, dtype=jnp.int32)
    phase = jnp.mod(freq_idx[None, :] * angle_idx[:, None], length).astype(jnp.float32) * (
        2.0 * math.pi / length
    )
    return jnp.concatenate([jnp.cos(phase), -jnp.sin(phase)], axis=1).astype(jnp.bfloat16)


def encode(block, w_mix, w_in, w_out):
    count, length, lanes = block.shape
    filters = w_mix.shape[1]
    freqs = w_in.shape[0] // filters
    angle_table = dft_table(length, freqs)
    spec = jnp.einsum("pac,ak->pkc", block, angle_table, preferred_element_type=jnp.float32).astype(
        jnp.bfloat16
    )
    mixed = jnp.dot(spec.reshape(-1, lanes), w_mix, preferred_element_type=jnp.float32).reshape(
        count, 2 * freqs, filters
    )
    real_part = mixed[:, :freqs]
    imag_part = mixed[:, freqs:]
    powers = real_part * real_part + imag_part * imag_part
    features = jnp.log1p(powers).reshape(count, -1)
    mean_removed = features - jnp.mean(features, axis=1, keepdims=True)
    reciprocal_scale = lax.rsqrt(
        jnp.mean(mean_removed * mean_removed, axis=1, keepdims=True) + 1e-05
    )
    normed = (mean_removed * reciprocal_scale).astype(jnp.bfloat16)
    preact = jnp.dot(normed, w_in, preferred_element_type=jnp.float32)
    hidden = jax.nn.silu(preact).astype(jnp.bfloat16)
    raw_embed = jnp.dot(hidden, w_out, preferred_element_type=jnp.float32)
    norms = jnp.sqrt(jnp.sum(raw_embed * raw_embed, axis=1, keepdims=True) + 1e-06)
    unit32 = raw_embed / norms
    saved = (
        spec,
        real_part,
        imag_part,
        powers,
        mean_removed,
        reciprocal_scale,
        normed,
        preact,
        hidden,
        unit32,
        norms,
    )
    return (unit32.astype(jnp.bfloat16), saved)


def back_upper(grad_units, saved, w_in, w_out):
    (
        spec,
        real_part,
        imag_part,
        powers,
        mean_removed,
        reciprocal_scale,
        normed,
        preact,
        hidden,
        unit32,
        norms,
    ) = saved
    grad_raw = (
        (grad_units - unit32 * jnp.sum(unit32 * grad_units, axis=1, keepdims=True)) / norms
    ).astype(jnp.bfloat16)
    g_out = jnp.dot(hidden.T, grad_raw, preferred_element_type=jnp.float32)
    grad_hid = jnp.dot(grad_raw, w_out.T, preferred_element_type=jnp.float32)
    sigm = jax.nn.sigmoid(preact)
    grad_pre = (grad_hid * sigm * (1.0 + preact * (1.0 - sigm))).astype(jnp.bfloat16)
    g_in = jnp.dot(normed.T, grad_pre, preferred_element_type=jnp.float32)
    norm_gradient = jnp.dot(grad_pre, w_in.T, preferred_element_type=jnp.float32)
    return (g_in, g_out, norm_gradient)


def back_lower(norm_gradient, saved):
    (
        spec,
        real_part,
        imag_part,
        powers,
        mean_removed,
        reciprocal_scale,
        normed,
        preact,
        hidden,
        unit32,
        norms,
    ) = saved
    lanes = spec.shape[2]
    normalized_input = mean_removed * reciprocal_scale
    feature_gradient = reciprocal_scale * (
        norm_gradient
        - jnp.mean(norm_gradient, axis=1, keepdims=True)
        - normalized_input * jnp.mean(norm_gradient * normalized_input, axis=1, keepdims=True)
    )
    grad_pow = feature_gradient.reshape(powers.shape) / (1.0 + powers)
    grad_mixed = jnp.concatenate(
        [2.0 * real_part * grad_pow, 2.0 * imag_part * grad_pow], axis=1
    ).astype(jnp.bfloat16)
    return jnp.dot(
        spec.reshape(-1, lanes).T,
        grad_mixed.reshape(-1, grad_mixed.shape[2]),
        preferred_element_type=jnp.float32,
    )


def negative_part(units, piece, row_ids):
    scores = SCALE * jnp.dot(units, piece.T, preferred_element_type=jnp.float32)
    column = jnp.arange(piece.shape[0], dtype=jnp.int32)
    expo = jnp.where(column[None, :] == row_ids[:, None], jnp.float32(0.0), jnp.exp(scores))
    return (
        jnp.sum(expo, axis=1),
        jnp.dot(expo.astype(jnp.bfloat16), piece, preferred_element_type=jnp.float32),
    )


def key_part(units, piece, tot_piece, row_ids):
    scores = SCALE * jnp.dot(piece, units.T, preferred_element_type=jnp.float32)
    column = jnp.arange(piece.shape[0], dtype=jnp.int32)
    expo = jnp.where(column[:, None] == row_ids[None, :], jnp.float32(0.0), jnp.exp(scores))
    weights = (expo / tot_piece[:, None]).astype(jnp.bfloat16)
    return jnp.dot(weights.T, piece, preferred_element_type=jnp.float32)


def on_device(patches, w_mix, w_in, w_out, partner_dev, partner_row):
    count = patches.shape[0]
    embed = w_out.shape[1]
    units, saved = encode(patches, w_mix, w_in, w_out)
    peers = lax.axis_size("dp")
    per_peer = count // peers
    sorted_positions = jnp.argsort(partner_dev, stable=True)
    inverse = jnp.argsort(sorted_positions, stable=True)
    wanted = partner_row[sorted_positions].reshape(peers, per_peer)
    asked = lax.all_to_all(wanted, "dp", split_axis=0, concat_axis=0, tiled=True)
    picked = units[asked]
    returned_rows = lax.all_to_all(picked, "dp", split_axis=0, concat_axis=0, tiled=True)
    positive = returned_rows.reshape(count, embed)[inverse]
    spos = SCALE * jnp.sum(units.astype(jnp.float32) * positive.astype(jnp.float32), axis=1)
    row_ids = lax.axis_index("blk") * count + jnp.arange(count, dtype=jnp.int32)
    zpart, npart = negative_part(units, lax.all_gather(units, "blk", axis=0, tiled=True), row_ids)
    totals = jnp.exp(spos) + zpart
    all_totals = lax.all_gather(totals, "blk", axis=0, tiled=True)
    keyterm = key_part(units, lax.all_gather(units, "blk", axis=0, tiled=True), all_totals, row_ids)
    loss_rows = jnp.log(totals) - spos
    coef = SCALE / count
    ppos = jnp.exp(spos) / totals
    partner_grad = coef * (ppos - 1.0)[:, None] * units.astype(jnp.float32)
    outgoing = partner_grad[sorted_positions].reshape(peers, per_peer, embed)
    incoming = lax.all_to_all(outgoing, "dp", split_axis=0, concat_axis=0, tiled=True)
    from_partner = (
        jnp.zeros((count, embed), jnp.float32)
        .at[asked.reshape(-1)]
        .add(incoming.reshape(-1, embed))
    )
    grad_units = (
        coef * ((ppos - 1.0)[:, None] * positive.astype(jnp.float32) + npart / totals[:, None])
        + coef * keyterm
        + from_partner
    )
    g_in, g_out, norm_gradient = back_upper(grad_units, saved, w_in, w_out)
    g_mix = back_lower(norm_gradient, saved)
    g_mix, g_in, g_out = lax.psum((g_mix, g_in, g_out), ("blk", "dp"))
    return (loss_rows, g_mix, g_in, g_out)


def solution(mesh):
    placed = (P(("blk", "dp"), None, None), P(), P(), P(), P(("blk", "dp")), P(("blk", "dp")))
    return jax.shard_map(
        on_device,
        mesh=mesh,
        in_specs=placed,
        out_specs=(P(("blk", "dp")), P(), P(), P()),
        check_vma=False,
    )
```

profile of v0, /device:TPU:0, one launch (start us, length us, event | category | flops | bytes accessed | tf_op | source)
XLA Modules:
  0.0 252.2 jit_solution(4154058484988354202)
XLA Ops:
  7.2 3.3 %sort.31 = (s32[128]{0:T(128)}, s32[128]{0:T(128)S(1)}) sort(s32[128]{0:T(128)} %param.10, s32[128]{0:T(128)S(1)} %iota.30), dimensions={0}, to_apply=%region_3.4 | sort | flops 896 | bytes 2048 | tf_op jit(solution)/shard_map/jit(argsort)/sort | solution.py:142
  10.5 1.6 gather_fusion
  12.8 6.4 %all-to-all-start = ((s32[8,1,16]{2,1,0:T(1,128)}), s32[8,1,16]{2,1,0:T(1,128)S(1)}, u32[]{:S(2)}, u32[]{:S(2)}) async-start(s32[8,1,16]{2,1,0:T(1,128)} %bitcast.4), calls=%async_computation | async-start | bytes 8192 | tf_op jit(solution)/shard_map/all_to_all | solution.py:145
  19.3 2.5 %sort.32 = (s32[128]{0:T(128)}, s32[128]{0:T(128)S(1)}) sort(s32[128]{0:T(128)S(1)} %get-tuple-element.6, s32[128]{0:T(128)S(1)} %iota.31), dimensions={0}, to_apply=%region_4.5 | sort | flops 896 | bytes 2048 | tf_op jit(solution)/shard_map/jit(argsort)/sort | solution.py:143
  21.8 2.9 %convert_bitcast_fusion = bf16[128,32,256]{2,1,0:T(8,128)(2,1)S(1)} fusion(bf16[128,64,256]{2,1,0:T(8,128)(2,1)} %param.6, bf16[64,16]{0,1:T(8,128)(2,1)S(1)} %get-tuple-element.27, bf16[64,16]{0,1:T(8,128)(2,1)S(1)} %get-tuple-element.28), kind=kOutput, calls=%fused_computation.7 | convolution fusion | flops 135274496 | bytes 6295552 | tf_op jit(solution)/shard_map/pac,ak->pkc/dot_general | solution.py:24
  24.8 2.5 fusion
  28.9 1.6 copy.38
  30.5 1.2 multiply_convert_fusion.2
  32.0 8.5 %all_gather.7 = bf16[512,128]{0,1:T(8,128)(2,1)S(1)} all-gather(bf16[128,128]{0,1:T(8,128)(2,1)S(1)} %fusion.35), channel_id=1, replica_groups=mesh['blk'=4,'dp'=8] {'blk'}, dimensions={0}, use_global_device_ids=true | all-gather | bytes 163840 | tf_op jit(solution)/shard_map/all_gather | solution.py:151
  42.9 1.3 gather_fusion.1
  44.2 5.1 %all-to-all-start.1 = ((bf16[8,16,128]{2,1,0:T(8,128)(2,1)}), bf16[8,16,128]{2,1,0:T(8,128)(2,1)S(1)}, u32[]{:S(2)}, u32[]{:S(2)}) async-start(bf16[8,16,128]{2,1,0:T(8,128)(2,1)} %bitcast.6), calls=%async_computation.1 | async-start | bytes 65536 | tf_op jit(solution)/shard_map/all_to_all | solution.py:147
  49.9 5.2 %all-to-all-done.1 = bf16[8,16,128]{2,1,0:T(8,128)(2,1)S(1)} async-done(((bf16[8,16,128]{2,1,0:T(8,128)(2,1)}), bf16[8,16,128]{2,1,0:T(8,128)(2,1)S(1)}, u32[]{:S(2)}, u32[]{:S(2)}) %all-to-all-start.1) | async-done | bytes 32800 | tf_op jit(solution)/shard_map/all_to_all | solution.py:147
  56.4 8.5 %all-gather = f32[4,1,128]{2,1,0:T(1,128)} all-gather(f32[1,1,128]{2,1,0:T(1,128)S(1)} %bitcast.47), channel_id=1, replica_groups=mesh['blk'=4,'dp'=8] {'blk'}, dimensions={0}, use_global_device_ids=true | all-gather | bytes 2560 | tf_op jit(solution)/shard_map/all_gather | solution.py:153
  65.1 1.2 gather_fusion.3
  66.3 3.5 %all-to-all-start.2 = ((f32[8,16,128]{2,1,0:T(8,128)}), f32[8,16,128]{2,1,0:T(8,128)S(1)}, u32[]{:S(2)}, u32[]{:S(2)}) async-start(f32[8,16,128]{2,1,0:T(8,128)} %bitcast.11), calls=%async_computation.2 | async-start | bytes 131072 | tf_op jit(solution)/shard_map/all_to_all | solution.py:160
  69.9 1.2 fusion.13
  71.0 2.0 fusion.12
  73.1 0.9 copy.45
  74.0 1.7 all-to-all-done.2
  75.7 1.5 scatter_fusion
  77.3 1.8 fusion.44
  79.1 1.2 fusion.9
  80.3 0.9 fusion.40
  81.2 2.8 %fusion.36 = f32[2048,512]{1,0:T(8,128)} fusion(bf16[128,512]{1,0:T(8,128)(2,1)S(1)} %fusion.9, f32[128,2048]{1,0:T(8,128)S(1)} %copy.38, f32[128]{0:T(128)S(1)} %add_rsqrt_fusion, f32[128]{0:T(128)S(1)} %broadcast_multiply_fusion.4), kind=kOutput, calls=%fused_computation.91 | convolution fusion | flops 269221888 | bytes 5374976 | tf_op jit(solution)/shard_map/dot_general | solution.py:81
  84.1 1.4 subtract_multiply_fusion
  85.5 1.5 copy.48
  87.0 2.0 multiply_convert_fusion.1
  89.1 1.7 copy.49
  90.8 3.3 %convolution_bitcast_fusion = f32[256,128]{1,0:T(8,128)} fusion(bf16[128,32,256]{2,1,0:T(8,128)(2,1)} %copy-done.3, bf16[128,32,128]{2,1,0:T(8,128)(2,1)} %copy.49), kind=kOutput, calls=%fused_computation.19 | convolution fusion | flops 268435456 | bytes 3276800 | tf_op jit(solution)/shard_map/dot_general | solution.py:111
  95.3 143.1 %all-reduce.3.cloned.1.call-done = (f32[256,128]{1,0:T(8,128)}, f32[2048,512]{1,0:T(8,128)}, f32[512,128]{1,0:T(8,128)}) async-done(((f32[256,128]{1,0:T(8,128)}, f32[2048,512]{1,0:T(8,128)}, f32[512,128]{1,0:T(8,128)}), (f32[256,128]{1,0:T(8,128)}, f32[2048,512]{1,0:T(8,128)}, f32[512,128]{1,0:T(8,128)})) %all-reduce.3.cloned.1.call-update) | async-done | bytes 4587536 | tf_op jit(solution)/shard_map/psum | solution.py:173
  238.4 1.6 copy.60
  239.9 4.7 %copy.61 = f32[2048,512]{1,0:T(8,128)} copy(f32[2048,512]{1,0:T(8,128)} %get-tuple-element.33) | data formatting | bytes 8388608
  (71 shorter events, 9.3 us)
Async XLA Ops:
  7.2 23.3 %copy-start = (bf16[2048,512]{1,0:T(8,128)(2,1)S(1)}, bf16[2048,512]{1,0:T(8,128)(2,1)}, u32[]{:S(2)}) copy-start(bf16[2048,512]{1,0:T(8,128)(2,1)} %param.8) | copy-start | bytes 6291460
  12.8 28.7 %all-to-all-start = ((s32[8,1,16]{2,1,0:T(1,128)}), s32[8,1,16]{2,1,0:T(1,128)S(1)}, u32[]{:S(2)}, u32[]{:S(2)}) async-start(s32[8,1,16]{2,1,0:T(1,128)} %bitcast.4), calls=%async_computation | async-start | bytes 8192 | tf_op jit(solution)/shard_map/all_to_all | solution.py:145
  19.2 21.2 %copy-start.14 = (s32[128]{0:T(128)}, s32[128]{0:T(128)S(1)}, u32[]{:S(2)}) copy-start(s32[128]{0:T(128)S(1)} %iota_add_fusion) | copy-start | bytes 1540
  21.8 2.9 %copy-start.8 = (bf16[256,128]{1,0:T(8,128)(2,1)S(1)}, bf16[256,128]{1,0:T(8,128)(2,1)}, u32[]{:S(2)}) copy-start(bf16[256,128]{1,0:T(8,128)(2,1)} %param.7) | copy-start | bytes 196612
  24.7 2.5 %copy-start.3 = (bf16[128,32,256]{2,1,0:T(8,128)(2,1)}, bf16[128,32,256]{2,1,0:T(8,128)(2,1)S(1)}, u32[]{:S(2)}) copy-start(bf16[128,32,256]{2,1,0:T(8,128)(2,1)S(1)} %convert_bitcast_fusion) | copy-start | bytes 6291460
  27.3 1.3 copy-start.1
  27.8 1.2 copy-start.2
  30.5 1.2 copy-start.5
  31.7 9.7 %copy-start.6 = (bf16[128,512]{1,0:T(8,128)(2,1)}, bf16[128,512]{1,0:T(8,128)(2,1)S(1)}, u32[]{:S(2)}) copy-start(bf16[128,512]{1,0:T(8,128)(2,1)S(1)} %get-tuple-element.20) | copy-start | bytes 393220
  40.5 0.9 copy-start.7
  44.2 10.8 %all-to-all-start.1 = ((bf16[8,16,128]{2,1,0:T(8,128)(2,1)}), bf16[8,16,128]{2,1,0:T(8,128)(2,1)S(1)}, u32[]{:S(2)}, u32[]{:S(2)}) async-start(bf16[8,16,128]{2,1,0:T(8,128)(2,1)} %bitcast.6), calls=%async_computation.1 | async-start | bytes 65536 | tf_op jit(solution)/shard_map/all_to_all | solution.py:147
  55.9 9.1 %copy-start.9 = (f32[128]{0:T(128)}, f32[128]{0:T(128)S(1)}, u32[]{:S(2)}) copy-start(f32[128]{0:T(128)S(1)} %fusion.21) | copy-start | bytes 1540
  56.4 8.6 %copy-start.11 = (f32[128]{0:T(128)}, f32[128]{0:T(128)S(1)}, u32[]{:S(2)}) copy-start(f32[128]{0:T(128)S(1)} %get-tuple-element.15) | copy-start | bytes 1540
  66.3 9.3 %copy-start.13 = (s32[128]{0:T(128)S(1)}, s32[128]{0:T(128)}, u32[]{:S(2)}) copy-start(s32[128]{0:T(128)} %fusion.31) | copy-start | bytes 1540
  66.3 9.3 %all-to-all-start.2 = ((f32[8,16,128]{2,1,0:T(8,128)}), f32[8,16,128]{2,1,0:T(8,128)S(1)}, u32[]{:S(2)}, u32[]{:S(2)}) async-start(f32[8,16,128]{2,1,0:T(8,128)} %bitcast.11), calls=%async_computation.2 | async-start | bytes 131072 | tf_op jit(solution)/shard_map/all_to_all | solution.py:160
  69.8 168.5 %all-reduce.3.cloned.1.call-start = ((), (), s32[]{:S(2)}) async-start(), calls=%async_computation.3 | async-start | bytes 9175040 | tf_op jit(solution)/shard_map/psum | solution.py:173
  94.1 0.7 copy-start.10
  94.1 0.7 copy-start.12
  239.9 4.7 %copy-start.4 = (f32[512,128]{1,0:T(8,128)S(1)}, f32[512,128]{1,0:T(8,128)}, u32[]{:S(2)}) copy-start(f32[512,128]{1,0:T(8,128)} %get-tuple-element.34) | copy-start | bytes 786436
Sparse Core Ops, SparseCore 0:
  94.2 144.0 all-reduce.2
where the time goes:
time: 253 us; the launch traced here: 252 us
  waiting for transfers between devices  150 us (59%)
  matrix products  21 us (8%)
  local copies, waits for them, and re-layouts  20.8 us (8%)
  blocking collectives  17 us (7%)
  starting transfers between devices  15 us (6%)
  between operations  14.3 us (6%)
  other arithmetic  14.1 us (6%)
    psum x1, waiting for transfers between devices, on_device(): g_mix, g_in, g_out = lax.psum((g_mix, g_in, g_out), ('blk', 'dp'))  143 us
    all_gather x1, blocking collectives, on_device(): all_totals = lax.all_gather(totals, 'blk', axis=0, tiled=True)  8.55 us
    unnamed x33, local copies, waits for them, and re-layouts  8.52 us
    all_gather x1, blocking collectives, on_device(): lax.all_gather(units, 'blk', axis=0, tiled=True)  8.46 us
    all_to_all x1, starting transfers between devices, on_device(): lax.all_to_all(wanted, 'dp', split_axis=0, concat_axis=0, tiled=True)  6.35 us
    all_to_all x1, waiting for transfers between devices, on_device(): lax.all_to_all(picked, 'dp', split_axis=0, concat_axis=0, tiled=True)  5.16 us
    all_to_all x1, starting transfers between devices, on_device(): lax.all_to_all(picked, 'dp', split_axis=0, concat_axis=0, tiled=True)  5.09 us
  transfers between devices with their start and end apart: 4, of which 3 were waited for; matrix products, arithmetic and copies ran while one was open for 7% of the time, Pallas kernels for 0%

commit v1 on v0

--- a/solution.py
+++ b/solution.py
@@ -170,7 +170,7 @@
     )
     g_in, g_out, norm_gradient = back_upper(grad_units, saved, w_in, w_out)
     g_mix = back_lower(norm_gradient, saved)
-    g_mix, g_in, g_out = lax.psum((g_mix, g_in, g_out), ("blk", "dp"))
+    g_mix, g_in, g_out = lax.psum(lax.psum((g_mix, g_in, g_out), "blk"), "dp")
     return (loss_rows, g_mix, g_in, g_out)
 
 

time: 253 us -> 324 us (1.28)
  waiting for transfers between devices: 150 us -> 221 us
    psum x1 -> x2, waiting for transfers between devices: 143 us -> 214 us  [on_device(): g_mix, g_in, g_out = lax.psum(lax.psum((g_mix, g_in, g_out), 'blk'), 'dp')]
  transfers between devices with their start and end apart: 4 -> 5, of which waited for: 3 -> 4; matrix products, arithmetic and copies ran while one was open for 7% -> 6% of each run, Pallas kernels for 0% -> 0%
where the time goes in v1:
time: 324 us
  waiting for transfers between devices  221 us (68%)
  matrix products  21 us (6%)
  local copies, waits for them, and re-layouts  20.8 us (6%)
  blocking collectives  17 us (5%)
  starting transfers between devices  15 us (5%)
  between operations  14.3 us (4%)
  other arithmetic  14.1 us (4%)
    psum x2, waiting for transfers between devices, on_device(): g_mix, g_in, g_out = lax.psum(lax.psum((g_mix, g_in, g_out), 'blk'), 'dp')  214 us
    all_gather x1, blocking collectives, on_device(): all_totals = lax.all_gather(totals, 'blk', axis=0, tiled=True)  8.54 us
    unnamed x33, local copies, waits for them, and re-layouts  8.49 us
    all_gather x1, blocking collectives, on_device(): lax.all_gather(units, 'blk', axis=0, tiled=True)  8.46 us
  transfers between devices with their start and end apart: 5, of which 4 were waited for; matrix products, arithmetic and copies ran while one was open for 6% of the time, Pallas kernels for 0%

profile of v1, /device:TPU:0, one launch (start us, length us, event | category | flops | bytes accessed | tf_op | source)
XLA Modules:
  0.0 323.5 jit_solution(4429578687611284516)
XLA Ops:
  7.2 3.3 %sort.31 = (s32[128]{0:T(128)}, s32[128]{0:T(128)S(1)}) sort(s32[128]{0:T(128)} %param.10, s32[128]{0:T(128)S(1)} %iota.30), dimensions={0}, to_apply=%region_3.4 | sort | flops 896 | bytes 2048 | tf_op jit(solution)/shard_map/jit(argsort)/sort | solution.py:142
  10.5 1.6 gather_fusion
  12.8 6.4 %all-to-all-start = ((s32[8,1,16]{2,1,0:T(1,128)}), s32[8,1,16]{2,1,0:T(1,128)S(1)}, u32[]{:S(2)}, u32[]{:S(2)}) async-start(s32[8,1,16]{2,1,0:T(1,128)} %bitcast.4), calls=%async_computation | async-start | bytes 8192 | tf_op jit(solution)/shard_map/all_to_all | solution.py:145
  19.3 2.5 sort.32
  21.8 2.9 convert_bitcast_fusion
  24.8 2.5 fusion
  28.9 1.6 copy.38
  30.5 1.2 multiply_convert_fusion.2
  32.0 8.5 %all_gather.7 = bf16[512,128]{0,1:T(8,128)(2,1)S(1)} all-gather(bf16[128,128]{0,1:T(8,128)(2,1)S(1)} %fusion.35), channel_id=1, replica_groups=mesh['blk'=4,'dp'=8] {'blk'}, dimensions={0}, use_global_device_ids=true | all-gather | bytes 163840 | tf_op jit(solution)/shard_map/all_gather | solution.py:151
  42.9 1.3 gather_fusion.1
  44.2 5.1 %all-to-all-start.1 = ((bf16[8,16,128]{2,1,0:T(8,128)(2,1)}), bf16[8,16,128]{2,1,0:T(8,128)(2,1)S(1)}, u32[]{:S(2)}, u32[]{:S(2)}) async-start(bf16[8,16,128]{2,1,0:T(8,128)(2,1)} %bitcast.6), calls=%async_computation.1 | async-start | bytes 65536 | tf_op jit(solution)/shard_map/all_to_all | solution.py:147
  49.9 5.2 %all-to-all-done.1 = bf16[8,16,128]{2,1,0:T(8,128)(2,1)S(1)} async-done(((bf16[8,16,128]{2,1,0:T(8,128)(2,1)}), bf16[8,16,128]{2,1,0:T(8,128)(2,1)S(1)}, u32[]{:S(2)}, u32[]{:S(2)}) %all-to-all-start.1) | async-done | bytes 32800 | tf_op jit(solution)/shard_map/all_to_all | solution.py:147
  56.4 8.5 %all-gather = f32[4,1,128]{2,1,0:T(1,128)} all-gather(f32[1,1,128]{2,1,0:T(1,128)S(1)} %bitcast.47), channel_id=1, replica_groups=mesh['blk'=4,'dp'=8] {'blk'}, dimensions={0}, use_global_device_ids=true | all-gather | bytes 2560 | tf_op jit(solution)/shard_map/all_gather | solution.py:153
  65.1 1.2 gather_fusion.3
  66.3 3.5 %all-to-all-start.2 = ((f32[8,16,128]{2,1,0:T(8,128)}), f32[8,16,128]{2,1,0:T(8,128)S(1)}, u32[]{:S(2)}, u32[]{:S(2)}) async-start(f32[8,16,128]{2,1,0:T(8,128)} %bitcast.11), calls=%async_computation.2 | async-start | bytes 131072 | tf_op jit(solution)/shard_map/all_to_all | solution.py:160
  69.9 1.2 fusion.13
  71.0 2.0 fusion.12
  73.1 0.9 copy.45
  74.0 1.7 all-to-all-done.2
  75.7 1.5 scatter_fusion
  77.3 1.8 fusion.44
  79.1 1.2 fusion.9
  81.2 2.8 fusion.36
  84.1 1.4 subtract_multiply_fusion
  85.5 1.5 copy.48
  87.1 2.0 multiply_convert_fusion.1
  89.1 1.7 copy.49
  90.8 3.3 %convolution_bitcast_fusion = f32[256,128]{1,0:T(8,128)} fusion(bf16[128,32,256]{2,1,0:T(8,128)(2,1)} %copy-done.3, bf16[128,32,128]{2,1,0:T(8,128)(2,1)} %copy.49), kind=kOutput, calls=%fused_computation.19 | convolution fusion | flops 268435456 | bytes 3276800 | tf_op jit(solution)/shard_map/dot_general | solution.py:111
  94.2 109.0 %all-reduce.7.cloned.1.call-done = (f32[256,128]{1,0:T(8,128)}, f32[2048,512]{1,0:T(8,128)}, f32[512,128]{1,0:T(8,128)}) async-done(((f32[256,128]{1,0:T(8,128)}, f32[2048,512]{1,0:T(8,128)}, f32[512,128]{1,0:T(8,128)}), (f32[256,128]{1,0:T(8,128)}, f32[2048,512]{1,0:T(8,128)}, f32[512,128]{1,0:T(8,128)})) %all-reduce.7.cloned.1.call-update) | async-done | bytes 4587536 | tf_op jit(solution)/shard_map/psum | solution.py:173
  204.3 105.4 %all-reduce.5.cloned.1.call-done = (f32[256,128]{1,0:T(8,128)}, f32[2048,512]{1,0:T(8,128)}, f32[512,128]{1,0:T(8,128)}) async-done(((f32[256,128]{1,0:T(8,128)}, f32[2048,512]{1,0:T(8,128)}, f32[512,128]{1,0:T(8,128)}), (f32[256,128]{1,0:T(8,128)}, f32[2048,512]{1,0:T(8,128)}, f32[512,128]{1,0:T(8,128)})) %all-reduce.5.cloned.1.call-update) | async-done | bytes 4587536 | tf_op jit(solution)/shard_map/psum | solution.py:173
  309.7 1.6 copy.63
  311.3 4.7 %copy.64 = f32[2048,512]{1,0:T(8,128)} copy(f32[2048,512]{1,0:T(8,128)} %get-tuple-element.36) | data formatting | bytes 8388608
  (74 shorter events, 10.3 us)
Async XLA Ops:
  7.2 23.3 %copy-start = (bf16[2048,512]{1,0:T(8,128)(2,1)S(1)}, bf16[2048,512]{1,0:T(8,128)(2,1)}, u32[]{:S(2)}) copy-start(bf16[2048,512]{1,0:T(8,128)(2,1)} %param.8) | copy-start | bytes 6291460
  12.8 28.7 %all-to-all-start = ((s32[8,1,16]{2,1,0:T(1,128)}), s32[8,1,16]{2,1,0:T(1,128)S(1)}, u32[]{:S(2)}, u32[]{:S(2)}) async-start(s32[8,1,16]{2,1,0:T(1,128)} %bitcast.4), calls=%async_computation | async-start | bytes 8192 | tf_op jit(solution)/shard_map/all_to_all | solution.py:145
  19.2 21.2 %copy-start.14 = (s32[128]{0:T(128)}, s32[128]{0:T(128)S(1)}, u32[]{:S(2)}) copy-start(s32[128]{0:T(128)S(1)} %iota_add_fusion) | copy-start | bytes 1540
  21.8 2.9 copy-start.8
  24.7 2.5 copy-start.3
  27.3 1.3 copy-start.1
  27.8 1.2 copy-start.2
  30.5 1.2 copy-start.5
  31.7 9.7 %copy-start.6 = (bf16[128,512]{1,0:T(8,128)(2,1)}, bf16[128,512]{1,0:T(8,128)(2,1)S(1)}, u32[]{:S(2)}) copy-start(bf16[128,512]{1,0:T(8,128)(2,1)S(1)} %get-tuple-element.23) | copy-start | bytes 393220
  40.5 0.9 copy-start.7
  44.2 10.8 %all-to-all-start.1 = ((bf16[8,16,128]{2,1,0:T(8,128)(2,1)}), bf16[8,16,128]{2,1,0:T(8,128)(2,1)S(1)}, u32[]{:S(2)}, u32[]{:S(2)}) async-start(bf16[8,16,128]{2,1,0:T(8,128)(2,1)} %bitcast.6), calls=%async_computation.1 | async-start | bytes 65536 | tf_op jit(solution)/shard_map/all_to_all | solution.py:147
  55.9 9.1 %copy-start.9 = (f32[128]{0:T(128)}, f32[128]{0:T(128)S(1)}, u32[]{:S(2)}) copy-start(f32[128]{0:T(128)S(1)} %fusion.21) | copy-start | bytes 1540
  56.4 8.6 %copy-start.11 = (f32[128]{0:T(128)}, f32[128]{0:T(128)S(1)}, u32[]{:S(2)}) copy-start(f32[128]{0:T(128)S(1)} %get-tuple-element.18) | copy-start | bytes 1540
  66.3 9.3 %copy-start.13 = (s32[128]{0:T(128)S(1)}, s32[128]{0:T(128)}, u32[]{:S(2)}) copy-start(s32[128]{0:T(128)} %fusion.31) | copy-start | bytes 1540
  66.3 9.3 %all-to-all-start.2 = ((f32[8,16,128]{2,1,0:T(8,128)}), f32[8,16,128]{2,1,0:T(8,128)S(1)}, u32[]{:S(2)}, u32[]{:S(2)}) async-start(f32[8,16,128]{2,1,0:T(8,128)} %bitcast.11), calls=%async_computation.2 | async-start | bytes 131072 | tf_op jit(solution)/shard_map/all_to_all | solution.py:160
  69.8 133.3 %all-reduce.7.cloned.1.call-start = ((), (), s32[]{:S(2)}) async-start(), calls=%async_computation.4 | async-start | bytes 9175040 | tf_op jit(solution)/shard_map/psum | solution.py:173
  94.1 215.6 %all-reduce.5.cloned.1.call-start = ((), (), s32[]{:S(2)}) async-start(), calls=%async_computation.3 | async-start | bytes 9175040 | tf_op jit(solution)/shard_map/psum | solution.py:173
  203.1 0.6 copy-start.10
  203.1 0.6 copy-start.12
  311.3 4.7 %copy-start.4 = (f32[512,128]{1,0:T(8,128)S(1)}, f32[512,128]{1,0:T(8,128)}, u32[]{:S(2)}) copy-start(f32[512,128]{1,0:T(8,128)} %get-tuple-element.37) | copy-start | bytes 786436
Sparse Core Ops, SparseCore 0:
  94.3 108.8 all-reduce.6
  205.7 103.9 all-reduce.4
